TPU v7x, 32 devices: a whole 2x2x4 slice. The times are simulated.
32 devices in a mesh: node: 8 (over z, core), edge: 4 (over y, x).
Axes of the slice: x: 2, y: 2, z: 4, core: 2. Of those that a mesh axis runs over, the one named last changes fastest.
Arguments:
- node_feats: bfloat16 [4096, 512], P(('node', 'edge')), may hold values from -40 to 40
- members: int32 [8, 4, 3072], P('node', None, 'edge'), may hold values from 0 to 511, as said below
- incidence_mask: int32 [8, 4, 3072], P('node', None, 'edge'), may hold values from 0 to 1
- degrees: int32 [3072], P(('edge', 'node')), may hold values from 0 to 32, as said below
- w_query: bfloat16 [512, 512], replicated, may hold values from -1 to 1
- w_key: bfloat16 [512, 512], replicated, may hold values from -1 to 1
- w_value: bfloat16 [512, 512], replicated, may hold values from -0.25 to 0.25
- w_out: bfloat16 [512, 512], replicated, may hold values from -0.5 to 0.5
Outputs:
- mixed: bfloat16 [3072, 512], P(('edge', 'node'))
Inputs may be any that keep to these rules, and one draw needn't show every extreme that they name: `members`: node index within the partition; only slots whose incidence_mask is 1 count. degrees[h] is the number of slots of hyperedge h over all partitions whose incidence_mask is 1; some hyperedge has every slot of every partition filled, and some hyperedge has none.
All inputs are finite; a program needn't handle non-finite values.
Results may differ from a plain program's by a relative error of at most 0.012.
Values may be sent and summed in bfloat16 or wider, within the bound.
No kernel may reach another device: no remote copies, remote signals or barrier semaphores. Data moves between devices by JAX's collectives and lax.ppermute only.
A program may use at most 64 MiB of HBM per device.

v0:
```python
import math
import jax
import jax.numpy as jnp
from jax import lax
from jax.sharding import PartitionSpec as P


def feature_map(values):
    return jax.nn.elu(values) + 1.0


def body(node_feats, members, incidence_mask, degrees, w_query, w_key, w_value, w_out):
    gathered = lax.all_gather(node_feats, "edge", axis=0, tiled=True)
    node_count = gathered.shape[0]
    width = gathered.shape[1]
    member_slots = members[0]
    slot_valid = incidence_mask[0]
    owned = degrees.shape[0]
    node_columns = lax.broadcasted_iota(jnp.int32, (1, node_count), 1)

    def block_term(first_row, block_size):
        slot_index = lax.dynamic_slice_in_dim(member_slots, first_row, block_size, 1)
        slot_keep = lax.dynamic_slice_in_dim(slot_valid, first_row, block_size, 1)
        counts = jnp.zeros((block_size, node_count), jnp.bfloat16)
        for slot in range(slot_index.shape[0]):
            hits = jnp.where(slot_index[slot][:, None] == node_columns, slot_keep[slot][:, None], 0)
            counts = counts + hits.astype(jnp.bfloat16)
        return jnp.dot(counts, gathered, preferred_element_type=jnp.float32)

    block_size = math.gcd(lax.axis_size("node") * owned, 512)
    block_total = lax.axis_size("node") * owned // block_size

    def block_rows(block):
        return block_term(block * block_size, block_size)

    stacked = lax.map(block_rows, jnp.arange(block_total, dtype=jnp.int32))
    hedge_sum = lax.psum_scatter(
        stacked.reshape(lax.axis_size("node") * owned, width).astype(jnp.bfloat16),
        "node",
        scatter_dimension=0,
        tiled=True,
    ).astype(jnp.float32)
    scale = jnp.maximum(degrees, 1).astype(jnp.float32)
    hedge = (hedge_sum / scale[:, None]).astype(jnp.bfloat16)
    query_proj = jnp.dot(hedge, w_query, preferred_element_type=jnp.float32)
    key_proj = jnp.dot(hedge, w_key, preferred_element_type=jnp.float32)
    value_proj = jnp.dot(hedge, w_value, preferred_element_type=jnp.float32)
    query_feats = feature_map(query_proj).astype(jnp.bfloat16)
    key_feats = feature_map(key_proj).astype(jnp.bfloat16)
    value_rows = value_proj.astype(jnp.bfloat16)
    gram_local = lax.dot_general(
        key_feats, value_rows, (((0,), (0,)), ((), ())), preferred_element_type=jnp.float32
    )
    key_local = jnp.sum(key_feats.astype(jnp.float32), axis=0)
    query_wide = query_feats.astype(jnp.float32)
    gram_whole, key_whole = lax.psum((gram_local, key_local), ("node", "edge"))
    numer = jnp.dot(query_wide, gram_whole, precision=lax.Precision.HIGHEST)
    denom = jnp.dot(query_wide, key_whole, precision=lax.Precision.HIGHEST)
    attended = (numer / denom[:, None]).astype(jnp.bfloat16)
    mixed = hedge.astype(jnp.float32) + jnp.dot(attended, w_out, preferred_element_type=jnp.float32)
    return mixed.astype(jnp.bfloat16)


def solution(mesh):
    placed = (
        P(("node", "edge"), None),
        P("node", None, "edge"),
        P("node", None, "edge"),
        P(("edge", "node")),
        P(),
        P(),
        P(),
        P(),
    )
    return jax.shard_map(
        body, mesh=mesh, in_specs=placed, out_specs=P(("edge", "node"), None), check_vma=False
    )
```

profile of v0, /device:TPU:0, one launch (start us, length us, event | category | flops | bytes accessed | tf_op | source)
XLA Modules:
  0.0 203.7 jit_solution(6001227106174851907)
XLA Ops:
  6.5 0.0 copy-start
  6.5 0.0 reduce-scatter.2.cloned.1.call-start
  6.5 12.0 %all_gather.3 = bf16[512,512]{1,0:T(8,128)(2,1)S(1)} all-gather(bf16[128,512]{1,0:T(8,128)(2,1)} %param.10), channel_id=1, replica_groups=mesh['node'=8,'edge'=4] {'edge'}, dimensions={0}, use_global_device_ids=true | all-gather | bytes 655360 | tf_op jit(solution)/shard_map/all_gather | solution.py:13
  18.5 8.1 %while.12 = (s32[]{:T(128)}, bf16[3,256,512]{2,1,0:T(8,128)(2,1)S(1)}, s32[3]{0:T(128)S(1)}, s32[4,768]{1,0:T(4,128)}, s32[4,768]{1,0:T(4,128)}, /*index=5*/bf16...) while((s32[]{:T(128)}, ...), condition=%wide.region_1.2_spmd.clone.clone, body=%wide.region_0.1_spmd.clone.clone.sunk | while | flops 136839168 | bytes 1073399 | solution.py:36
  18.5 0.6 dynamic_slice.17
  19.8 0.9 constant_dynamic-slice_fusion.3
  20.7 0.5 fusion.46
  21.3 0.6 dynamic_slice.17
  22.5 0.9 constant_dynamic-slice_fusion.3
  23.4 0.5 fusion.46
  24.0 0.6 dynamic_slice.17
  25.2 0.9 constant_dynamic-slice_fusion.3
  26.1 0.5 fusion.46
  26.7 0.0 copy-start.1
  26.7 0.0 copy-start.3
  26.7 0.0 copy-start.6
  26.7 0.9 copy-done.1
  27.6 0.0 reduce-scatter.2.cloned.1.call-update
  27.6 0.0 all-reduce.2.cloned.1.call-start
  27.6 0.0 copy-done.6
  27.7 32.2 %reduce-scatter.2.cloned.1.call-done = bf16[96,512]{1,0:T(8,128)(2,1)} async-done(((bf16[768,512]{1,0:T(8,128)(2,1)}), bf16[96,512]{1,0:T(8,128)(2,1)}) %reduce-scatter.2.cloned.1.call-update) | async-done | bytes 98320 | tf_op jit(solution)/shard_map/reduce_scatter | solution.py:37
  59.9 0.0 copy-done.3
  59.9 0.0 copy-start.2
  59.9 1.3 convert_reduce_fusion
  61.2 0.0 copy-done
  61.2 0.0 copy-done.2
  61.2 1.5 fusion.19
  62.7 0.0 copy-start.4
  62.8 0.0 all-reduce.2.cloned.1.call-update
  62.8 38.2 %psum.15 = f32[512]{0:T(512)S(1)} all-reduce(f32[512]{0:T(512)S(1)} %get-tuple-element.110), channel_id=1, replica_groups=mesh['node'=8,'edge'=4] {'node','edge'}, use_global_device_ids=true, to_apply=%region_5.6 | all-reduce | flops 512 | bytes 4096 | tf_op jit(solution)/shard_map/psum | solution.py:56
  100.9 0.0 copy-done.4
  101.0 0.3 fusion.32
  101.2 0.2 convolution_bitcast_fusion.1
  101.4 0.0 copy-start.5
  101.4 92.8 %all-reduce.2.cloned.1.call-done = f32[512,512]{1,0:T(8,128)} async-done(((f32[512,512]{1,0:T(8,128)}), f32[512,512]{1,0:T(8,128)}) %all-reduce.2.cloned.1.call-update) | async-done | bytes 1048592 | tf_op jit(solution)/shard_map/psum | solution.py:56
  194.2 1.8 fusion.17
  196.0 0.0 copy-done.5
  196.0 0.9 fusion.18
  (3 shorter events, 0.0 us)
Async XLA Ops:
  6.5 54.7 %copy-start = (bf16[512,512]{1,0:T(8,128)(2,1)S(1)}, bf16[512,512]{1,0:T(8,128)(2,1)}, u32[]{:S(2)}) copy-start(bf16[512,512]{1,0:T(8,128)(2,1)} %param.16) | copy-start | bytes 1572868
  6.5 53.3 %reduce-scatter.2.cloned.1.call-start = ((), (), s32[]{:S(2)}) async-start(), calls=%async_computation.1 | async-start | bytes 884736 | tf_op jit(solution)/shard_map/reduce_scatter | solution.py:37
  26.7 0.9 copy-start.1
  26.7 33.2 %copy-start.3 = (bf16[512,512]{1,0:T(8,128)(2,1)S(1)}, bf16[512,512]{1,0:T(8,128)(2,1)}, u32[]{:S(2)}) copy-start(bf16[512,512]{1,0:T(8,128)(2,1)} %param.15) | copy-start | bytes 1572868
  26.7 0.9 copy-start.6
  27.6 166.6 %all-reduce.2.cloned.1.call-start = ((), (), s32[]{:S(2)}) async-start(), calls=%async_computation.2 | async-start | bytes 2097152 | tf_op jit(solution)/shard_map/psum | solution.py:56
  59.9 1.3 copy-start.2
  62.7 38.2 %copy-start.4 = (bf16[512,512]{1,0:T(8,128)(2,1)S(1)}, bf16[512,512]{1,0:T(8,128)(2,1)}, u32[]{:S(2)}) copy-start(bf16[512,512]{1,0:T(8,128)(2,1)} %param.14) | copy-start | bytes 1572868
  101.4 94.6 %copy-start.5 = (bf16[512,512]{1,0:T(8,128)(2,1)S(1)}, bf16[512,512]{1,0:T(8,128)(2,1)}, u32[]{:S(2)}) copy-start(bf16[512,512]{1,0:T(8,128)(2,1)} %param.17) | copy-start | bytes 1572868
Sparse Core Ops, SparseCore 0:
  27.7 32.1 reduce-scatter.1
  65.1 129.1 all-reduce.1
where the time goes:
time: 204 us
  waiting for transfers between devices  125 us (61%)
  blocking collectives  50.2 us (25%)
  between operations  13.5 us (7%)
  matrix products  7.58 us (4%)
  local copies, waits for them, and re-layouts  5.46 us (3%)
    psum x1, waiting for transfers between devices, body(): gram_whole, key_whole = lax.psum((gram_local, key_local), ('node', 'edge'))  92.8 us
    psum x1, blocking collectives, body(): gram_whole, key_whole = lax.psum((gram_local, key_local), ('node', 'edge'))  38.2 us
    reduce_scatter x1, waiting for transfers between devices, body(): lax.psum_scatter(stacked.reshape(lax.axis_size('node') * owned, width).as...  32.2 us
    all_gather x1, blocking collectives, body(): gathered = lax.all_gather(node_feats, 'edge', axis=0, tiled=True)  12 us
  transfers between devices with their start and end apart: 2, of which 2 were waited for; matrix products, arithmetic and copies ran while one was open for 0% of the time, Pallas kernels for 0%

commit v1 on v0

--- a/solution.py
+++ b/solution.py
@@ -1,8 +1,16 @@
+import functools
 import math
 import jax
 import jax.numpy as jnp
 from jax import lax
 from jax.sharding import PartitionSpec as P
+
+
+def sample_play(x0, which_axis, axis_tag):
+    return lax.psum(lax.psum(x0, axis_name=which_axis), axis_name=axis_tag)
+
+
+wrap_turns = functools.partial(sample_play, which_axis="edge", axis_tag="node")
 
 
 def feature_map(values):
@@ -53,7 +61,7 @@
     )
     key_local = jnp.sum(key_feats.astype(jnp.float32), axis=0)
     query_wide = query_feats.astype(jnp.float32)
-    gram_whole, key_whole = lax.psum((gram_local, key_local), ("node", "edge"))
+    gram_whole, key_whole = wrap_turns((gram_local, key_local))
     numer = jnp.dot(query_wide, gram_whole, precision=lax.Precision.HIGHEST)
     denom = jnp.dot(query_wide, key_whole, precision=lax.Precision.HIGHEST)
     attended = (numer / denom[:, None]).astype(jnp.bfloat16)

time: 204 us -> 185 us (0.907)
  blocking collectives: 50.2 us -> 35.4 us
  waiting for transfers between devices: 125 us -> 121 us
    psum x1 -> x2, blocking collectives: 38.2 us -> 23.5 us  [sample_play(): return lax.psum(lax.psum(x0, axis_name=which_axis), axis_name=axis_tag)]
    psum x1 -> x2, waiting for transfers between devices: 92.8 us -> 88.7 us  [sample_play(): return lax.psum(lax.psum(x0, axis_name=which_axis), axis_name=axis_tag)]
  transfers between devices with their start and end apart: 2 -> 3, of which waited for: 2 -> 3; matrix products, arithmetic and copies ran while one was open for 0% -> 0% of each run, Pallas kernels for 0% -> 0%
where the time goes in v1:
time: 185 us
  waiting for transfers between devices  121 us (65%)
  blocking collectives  35.4 us (19%)
  between operations  13.2 us (7%)
  matrix products  7.59 us (4%)
  local copies, waits for them, and re-layouts  5.51 us (3%)
  loops' own time  2 us (1%)
    psum x2, waiting for transfers between devices, sample_play(): return lax.psum(lax.psum(x0, axis_name=which_axis), axis_name=axis_tag)  88.7 us
    reduce_scatter x1, waiting for transfers between devices, body(): lax.psum_scatter(stacked.reshape(lax.axis_size('node') * owned, width).as...  32.2 us
    psum x2, blocking collectives, sample_play(): return lax.psum(lax.psum(x0, axis_name=which_axis), axis_name=axis_tag)  23.5 us
    all_gather x1, blocking collectives, body(): gathered = lax.all_gather(node_feats, 'edge', axis=0, tiled=True)  12 us
  transfers between devices with their start and end apart: 3, of which 3 were waited for; matrix products, arithmetic and copies ran while one was open for 0% of the time, Pallas kernels for 0%

profile of v1, /device:TPU:0, one launch (start us, length us, event | category | flops | bytes accessed | tf_op | source)
XLA Modules:
  0.0 184.7 jit_solution(4290078687317774802)
XLA Ops:
  6.5 0.0 copy-start
  6.5 0.0 reduce-scatter.2.cloned.1.call-start
  6.5 12.0 %all_gather.3 = bf16[512,512]{1,0:T(8,128)(2,1)S(1)} all-gather(bf16[128,512]{1,0:T(8,128)(2,1)} %param.10), channel_id=1, replica_groups=mesh['node'=8,'edge'=4] {'edge'}, dimensions={0}, use_global_device_ids=true | all-gather | bytes 655360 | tf_op jit(solution)/shard_map/all_gather | solution.py:21
  18.5 8.2 %while.12 = (s32[]{:T(128)}, bf16[3,256,512]{2,1,0:T(8,128)(2,1)S(1)}, s32[3]{0:T(128)S(1)}, s32[4,768]{1,0:T(4,128)}, s32[4,768]{1,0:T(4,128)}, /*index=5*/bf16...) while((s32[]{:T(128)}, ...), condition=%wide.region_1.2_spmd.clone.clone, body=%wide.region_0.1_spmd.clone.clone.sunk | while | flops 136839168 | bytes 1073399 | solution.py:44
  18.5 0.6 dynamic_slice.17
  19.8 0.9 constant_dynamic-slice_fusion.3
  20.7 0.5 fusion.46
  21.3 0.6 dynamic_slice.17
  22.5 0.9 constant_dynamic-slice_fusion.3
  23.5 0.5 fusion.46
  24.0 0.6 dynamic_slice.17
  25.3 0.9 constant_dynamic-slice_fusion.3
  26.2 0.5 fusion.46
  26.8 0.0 copy-start.1
  26.8 0.0 copy-start.3
  26.8 0.0 copy-start.6
  26.8 0.8 copy-done.1
  27.7 0.0 reduce-scatter.2.cloned.1.call-update
  27.7 0.0 all-reduce.3.cloned.1.call-start
  27.7 0.0 copy-done.6
  27.8 32.2 %reduce-scatter.2.cloned.1.call-done = bf16[96,512]{1,0:T(8,128)(2,1)} async-done(((bf16[768,512]{1,0:T(8,128)(2,1)}), bf16[96,512]{1,0:T(8,128)(2,1)}) %reduce-scatter.2.cloned.1.call-update) | async-done | bytes 98320 | tf_op jit(solution)/shard_map/reduce_scatter | solution.py:45
  60.0 0.0 copy-done.3
  60.0 0.0 copy-start.2
  60.0 1.3 convert_reduce_fusion
  61.3 0.0 copy-done
  61.3 0.0 copy-done.2
  61.3 1.6 fusion.19
  62.9 0.0 all-reduce.3.cloned.1.call-update
  62.9 0.0 all-reduce.5.cloned.1.call-start
  62.9 50.9 %all-reduce.3.cloned.1.call-done = f32[512,512]{1,0:T(8,128)} async-done(((f32[512,512]{1,0:T(8,128)}), f32[512,512]{1,0:T(8,128)}) %all-reduce.3.cloned.1.call-update) | async-done | bytes 1048592 | tf_op jit(solution)/shard_map/psum | solution.py:10
  113.8 0.0 copy-start.4
  113.8 0.0 all-reduce.5.cloned.1.call-update
  113.9 9.1 %psum.30 = f32[512]{0:T(512)S(1)} all-reduce(f32[512]{0:T(512)S(1)} %get-tuple-element.110), channel_id=1, replica_groups=mesh['node'=8,'edge'=4] {'edge'}, use_global_device_ids=true, to_apply=%region_6.7 | all-reduce | flops 512 | bytes 4096 | tf_op jit(solution)/shard_map/psum | solution.py:10
  122.9 14.4 %psum.31 = f32[512]{0:T(512)S(1)} all-reduce(f32[512]{0:T(512)S(1)} %psum.30), channel_id=1, replica_groups=mesh['node'=8,'edge'=4] {'node'}, use_global_device_ids=true, to_apply=%region_7.8 | all-reduce | flops 512 | bytes 4096 | tf_op jit(solution)/shard_map/psum | solution.py:10
  137.3 0.0 copy-done.4
  137.3 0.3 fusion.32
  137.6 0.2 convolution_bitcast_fusion.1
  137.8 0.0 copy-start.5
  137.8 37.8 %all-reduce.5.cloned.1.call-done = f32[512,512]{1,0:T(8,128)} async-done(((f32[512,512]{1,0:T(8,128)}), f32[512,512]{1,0:T(8,128)}) %all-reduce.5.cloned.1.call-update) | async-done | bytes 1048592 | tf_op jit(solution)/shard_map/psum | solution.py:10
  175.5 1.8 fusion.17
  177.3 0.0 copy-done.5
  177.3 0.9 fusion.18
  (3 shorter events, 0.0 us)
Async XLA Ops:
  6.5 54.7 %copy-start = (bf16[512,512]{1,0:T(8,128)(2,1)S(1)}, bf16[512,512]{1,0:T(8,128)(2,1)}, u32[]{:S(2)}) copy-start(bf16[512,512]{1,0:T(8,128)(2,1)} %param.16) | copy-start | bytes 1572868
  6.5 53.4 %reduce-scatter.2.cloned.1.call-start = ((), (), s32[]{:S(2)}) async-start(), calls=%async_computation.1 | async-start | bytes 884736 | tf_op jit(solution)/shard_map/reduce_scatter | solution.py:45
  26.8 0.9 copy-start.1
  26.8 33.2 %copy-start.3 = (bf16[512,512]{1,0:T(8,128)(2,1)S(1)}, bf16[512,512]{1,0:T(8,128)(2,1)}, u32[]{:S(2)}) copy-start(bf16[512,512]{1,0:T(8,128)(2,1)} %param.15) | copy-start | bytes 1572868
  26.8 0.9 copy-start.6
  27.7 86.2 %all-reduce.3.cloned.1.call-start = ((), (), s32[]{:S(2)}) async-start(), calls=%async_computation.2 | async-start | bytes 2097152 | tf_op jit(solution)/shard_map/psum | solution.py:10
  60.0 1.3 copy-start.2
  62.9 112.7 %all-reduce.5.cloned.1.call-start = ((), (), s32[]{:S(2)}) async-start(), calls=%async_computation.3 | async-start | bytes 2097152 | tf_op jit(solution)/shard_map/psum | solution.py:10
  113.8 23.5 %copy-start.4 = (bf16[512,512]{1,0:T(8,128)(2,1)S(1)}, bf16[512,512]{1,0:T(8,128)(2,1)}, u32[]{:S(2)}) copy-start(bf16[512,512]{1,0:T(8,128)(2,1)} %param.14) | copy-start | bytes 1572868
  137.8 39.6 %copy-start.5 = (bf16[512,512]{1,0:T(8,128)(2,1)S(1)}, bf16[512,512]{1,0:T(8,128)(2,1)}, u32[]{:S(2)}) copy-start(bf16[512,512]{1,0:T(8,128)(2,1)} %param.17) | copy-start | bytes 1572868
Sparse Core Ops, SparseCore 0:
  27.8 32.1 reduce-scatter.1
  63.0 50.7 all-reduce.2
  116.2 59.2 all-reduce.4
